TPU v7x, 32 devices: a whole 2x2x4 slice. The times are simulated.
32 devices in a mesh: ctx: 4 (over z), fsdp: 8 (over y, x, core).
Axes of the slice: x: 2, y: 2, z: 4, core: 2. Of those that a mesh axis runs over, the one named last changes fastest.
Arguments:
- tokens: bfloat16 [8, 512, 1024], P('fsdp', 'ctx'), may hold values from -12 to 12
- cotangent: bfloat16 [8, 512, 1024], P('fsdp', 'ctx'), may hold values from -6 to 6
- weight_rows: float32 [12288, 1024], P('fsdp'), may hold values from -2 to 2
- first_rows: float32 [12288, 1024], P('fsdp')
- second_rows: float32 [12288, 1024], P('fsdp'), as said below
- vector_rows: float32 [12, 1024], replicated, may hold values from -2 to 2
- vector_first: float32 [12, 1024], replicated
- vector_second: float32 [12, 1024], replicated, as said below
Outputs:
- output: bfloat16 [8, 512, 1024], P('fsdp', 'ctx')
- input_grad: float32 [8, 512, 1024], P('fsdp', 'ctx')
- weight_grad: float32 [12288, 1024], P('fsdp')
- new_weights: float32 [12288, 1024], P('fsdp')
- new_first: float32 [12288, 1024], P('fsdp')
- new_second: float32 [12288, 1024], P('fsdp')
- vector_grad: float32 [12, 1024], replicated
- new_vectors: float32 [12, 1024], replicated
- new_vector_first: float32 [12, 1024], replicated
- new_vector_second: float32 [12, 1024], replicated
Inputs may be any that keep to these rules, and one draw needn't show every extreme that they name: `second_rows`: every entry is positive. `vector_second`: every entry is positive.
All inputs are finite; a program needn't handle non-finite values.
Results may differ from a plain program's by a relative error of at most 0.025.
The roundings to bfloat16 on the way count: a program that leaves them out, or rounds other values in their place, can miss the bound.
Values may be sent and summed in bfloat16 or wider, within the bound.
No kernel may reach another device: no remote copies, remote signals or barrier semaphores. Data moves between devices by JAX's collectives and lax.ppermute only.
A program may use at most 320 MiB of HBM per device.

v0:
```python
import math
import jax
import jax.numpy as jnp
from jax import lax
from jax.sharding import PartitionSpec as P

D = 1024
HEADS = 16
beta_one = 0.9
beta_two = 0.999
learn_rate = 0.01
decay_rate = 0.01
adam_eps = 1e-08
norm_eps = 1e-05
adam_step = 2


def mat_nt(left, right):
    return lax.dot_general(
        left, right, (((1,), (1,)), ((), ())), preferred_element_type=jnp.float32
    )


def mat_tn(left, right):
    return lax.dot_general(
        left, right, (((0,), (0,)), ((), ())), preferred_element_type=jnp.float32
    )


def unpack(rows, vectors):
    width = rows.shape[1]
    hidden = (rows.shape[0] - 4 * width) // 2
    return [
        rows[: 3 * width],
        vectors[0],
        vectors[1],
        rows[3 * width : 4 * width],
        vectors[2],
        vectors[3],
        vectors[4],
        rows[4 * width : 4 * width + hidden],
        vectors[8:].reshape(hidden),
        rows[4 * width + hidden :],
        vectors[5],
        vectors[6],
        vectors[7],
    ]


def normalize(values):
    centred = values - jnp.mean(values, axis=-1, keepdims=True)
    inverse = lax.rsqrt(jnp.mean(centred * centred, axis=-1, keepdims=True) + norm_eps)
    return (centred * inverse, inverse)


def norm_back(grad_norm, normed, inverse):
    return inverse * (
        grad_norm
        - jnp.mean(grad_norm, axis=-1, keepdims=True)
        - normed * jnp.mean(grad_norm * normed, axis=-1, keepdims=True)
    )


def gelu_grad(pre_act):
    return (
        0.5 * (1.0 + lax.erf(pre_act * 0.7071067811865476))
        + pre_act * jnp.exp(-0.5 * pre_act * pre_act) * 0.3989422804014327
    )


def project(inputs, params):
    qkv_t, query_b, value_b = (params[0], params[1], params[2])
    width = qkv_t.shape[1]
    projected = mat_nt(inputs, qkv_t)
    query_rows = (projected[:, :width] + query_b.astype(jnp.float32)).astype(jnp.bfloat16)
    key_rows = projected[:, width : 2 * width].astype(jnp.bfloat16)
    value_rows = (projected[:, 2 * width :] + value_b.astype(jnp.float32)).astype(jnp.bfloat16)
    return (query_rows, key_rows, value_rows)


def tail_forward(inputs, attended, params):
    out_t, out_b, gain_one, shift_one, up_t, up_b, down_w, down_b, gain_two, shift_two = params[3:]
    first_sum = inputs.astype(jnp.float32) + mat_nt(attended, out_t) + out_b.astype(jnp.float32)
    normed_one, inverse_one = normalize(first_sum)
    hidden_in = normed_one * gain_one.astype(jnp.float32) + shift_one.astype(jnp.float32)
    hidden_b = hidden_in.astype(jnp.bfloat16)
    pre_act = mat_nt(hidden_b, up_t) + up_b.astype(jnp.float32)
    activ_b = jax.nn.gelu(pre_act, approximate=False).astype(jnp.bfloat16)
    second_sum = (
        hidden_in
        + jnp.dot(activ_b, down_w, preferred_element_type=jnp.float32)
        + down_b.astype(jnp.float32)
    )
    normed_two, inverse_two = normalize(second_sum)
    output = (normed_two * gain_two.astype(jnp.float32) + shift_two.astype(jnp.float32)).astype(
        jnp.bfloat16
    )
    return (output, (normed_one, inverse_one, hidden_b, pre_act, activ_b, normed_two, inverse_two))


def tail_backward(cotan, attended, saved, params):
    out_t, out_b, gain_one, shift_one, up_t, up_b, down_w, down_b, gain_two, shift_two = params[3:]
    normed_one, inverse_one, hidden_b, pre_act, activ_b, normed_two, inverse_two = saved
    grad_gain_two = jnp.sum(cotan * normed_two, axis=0)
    grad_shift_two = jnp.sum(cotan, axis=0)
    grad_second = norm_back(cotan * gain_two.astype(jnp.float32), normed_two, inverse_two)
    grad_second_b = grad_second.astype(jnp.bfloat16)
    grad_down_b = jnp.sum(grad_second, axis=0)
    grad_down_w = mat_tn(activ_b, grad_second_b)
    grad_pre = mat_nt(grad_second_b, down_w) * gelu_grad(pre_act)
    grad_pre_b = grad_pre.astype(jnp.bfloat16)
    grad_up_b = jnp.sum(grad_pre, axis=0)
    grad_up_t = mat_tn(grad_pre_b, hidden_b)
    grad_hidden = grad_second + jnp.dot(grad_pre_b, up_t, preferred_element_type=jnp.float32)
    grad_gain_one = jnp.sum(grad_hidden * normed_one, axis=0)
    grad_shift_one = jnp.sum(grad_hidden, axis=0)
    grad_first = norm_back(grad_hidden * gain_one.astype(jnp.float32), normed_one, inverse_one)
    grad_first_b = grad_first.astype(jnp.bfloat16)
    grad_out_b = jnp.sum(grad_first, axis=0)
    grad_out_t = mat_tn(grad_first_b, attended)
    grad_attended = jnp.dot(grad_first_b, out_t, preferred_element_type=jnp.float32).astype(
        jnp.bfloat16
    )
    tail_grads = (
        grad_out_t,
        grad_out_b,
        grad_gain_one,
        grad_shift_one,
        grad_up_t,
        grad_up_b,
        grad_down_w,
        grad_down_b,
        grad_gain_two,
        grad_shift_two,
    )
    return (grad_first, grad_attended, tail_grads)


def head_backward(inputs, grad_first, grad_query, grad_key, grad_value, qkv_t):
    grad_proj_b = jnp.concatenate([grad_query, grad_key, grad_value], axis=1).astype(jnp.bfloat16)
    grad_qkv_t = mat_tn(grad_proj_b, inputs)
    grad_inputs = grad_first + jnp.dot(grad_proj_b, qkv_t, preferred_element_type=jnp.float32)
    return (grad_inputs, grad_qkv_t, jnp.sum(grad_query, axis=0), jnp.sum(grad_value, axis=0))


def pack_grads(grad_qkv_t, grad_query_b, grad_value_b, tail_grads):
    width = grad_qkv_t.shape[1]
    matrix = jnp.concatenate([grad_qkv_t, tail_grads[0], tail_grads[4], tail_grads[6]], axis=0)
    small = jnp.stack(
        [
            grad_query_b,
            grad_value_b,
            tail_grads[1],
            tail_grads[2],
            tail_grads[3],
            tail_grads[7],
            tail_grads[8],
            tail_grads[9],
        ]
    )
    vectors = jnp.concatenate([small, tail_grads[5].reshape(-1, width)], axis=0)
    return (matrix, vectors)


def adam_update(weights, grads, first, second):
    first_new = beta_one * first + (1.0 - beta_one) * grads
    second_new = beta_two * second + (1.0 - beta_two) * grads * grads
    first_hat = first_new / (1.0 - beta_one**adam_step)
    second_hat = second_new / (1.0 - beta_two**adam_step)
    weights_new = weights - learn_rate * (
        first_hat / (jnp.sqrt(second_hat) + adam_eps) + decay_rate * weights
    )
    return (weights_new, first_new, second_new)


def split_heads(matrix):
    return matrix.reshape(matrix.shape[0], HEADS, matrix.shape[1] // HEADS)


def local(
    tokens,
    cotangent,
    weight_rows,
    first_rows,
    second_rows,
    vector_rows,
    vector_first,
    vector_second,
):
    row_count = tokens.shape[1]
    inputs = tokens.reshape(row_count, D)
    cotan = cotangent.reshape(row_count, D).astype(jnp.float32)
    head_width = D // HEADS
    score_scale = 1.0 / math.sqrt(head_width)
    vectors_b = vector_rows.astype(jnp.bfloat16)
    gathered = lax.all_gather(weight_rows.astype(jnp.bfloat16), "fsdp", axis=0, tiled=True)
    params = unpack(gathered, vectors_b)
    query_rows, key_rows, value_rows = project(inputs, params)
    query_heads = split_heads(query_rows)
    start_state = (
        jnp.full((HEADS, row_count), -jnp.inf, jnp.float32),
        jnp.zeros((HEADS, row_count), jnp.float32),
        jnp.zeros((HEADS, row_count, head_width), jnp.float32),
    )
    key_piece = lax.all_gather(key_rows, "ctx", axis=0, tiled=True)
    value_piece = lax.all_gather(value_rows, "ctx", axis=0, tiled=True)
    amount = key_piece.shape[0]
    block_rows = math.gcd(amount, 512)

    def one_block(position, running):
        row_top, row_total, weighted = running
        key_block = split_heads(
            lax.dynamic_slice_in_dim(key_piece, position * block_rows, block_rows, 0)
        )
        value_block = split_heads(
            lax.dynamic_slice_in_dim(value_piece, position * block_rows, block_rows, 0)
        ).astype(jnp.float32)
        scores = (
            jnp.einsum("qhd,khd->hqk", query_heads, key_block, preferred_element_type=jnp.float32)
            * score_scale
        )
        new_top = jnp.maximum(row_top, jnp.max(scores, axis=-1))
        rescale = jnp.exp(row_top - new_top)
        weights = jnp.exp(scores - new_top[:, :, None])
        row_total = row_total * rescale + jnp.sum(weights, axis=-1)
        weighted = weighted * rescale[:, :, None] + jnp.einsum(
            "hqk,khd->hqd", weights, value_block, precision=lax.Precision.HIGHEST
        )
        return (new_top, row_total, weighted)

    row_top, row_total, weighted = lax.fori_loop(0, amount // block_rows, one_block, start_state)
    attended = (
        (weighted / row_total[:, :, None])
        .transpose(1, 0, 2)
        .reshape(row_count, D)
        .astype(jnp.bfloat16)
    )
    log_totals = row_top + jnp.log(row_total)
    output, saved = tail_forward(inputs, attended, params)
    grad_first, grad_attended, tail_grads = tail_backward(cotan, attended, saved, params)
    grad_heads = split_heads(grad_attended)
    delta = jnp.sum(
        grad_heads.astype(jnp.float32) * split_heads(attended).astype(jnp.float32), axis=-1
    ).T
    seq_length = row_count * lax.axis_size("ctx")
    back_state = (
        jnp.zeros((row_count, HEADS, head_width), jnp.float32),
        jnp.zeros((seq_length, D), jnp.float32),
        jnp.zeros((seq_length, D), jnp.float32),
    )
    attend_key_piece = lax.all_gather(key_rows, "ctx", axis=0, tiled=True)
    attend_value_piece = lax.all_gather(value_rows, "ctx", axis=0, tiled=True)
    amount = attend_key_piece.shape[0]
    attend_block_rows = math.gcd(amount, 512)

    def one_block(position, running):
        grad_query, grad_key, grad_value = running
        offset = position * attend_block_rows
        key_block = split_heads(
            lax.dynamic_slice_in_dim(attend_key_piece, offset, attend_block_rows, 0)
        )
        value_block = split_heads(
            lax.dynamic_slice_in_dim(attend_value_piece, offset, attend_block_rows, 0)
        )
        scores = (
            jnp.einsum("qhd,khd->hqk", query_heads, key_block, preferred_element_type=jnp.float32)
            * score_scale
        )
        probs = jnp.exp(scores - log_totals[:, :, None])
        grad_probs = jnp.einsum(
            "qhd,khd->hqk", grad_heads, value_block, preferred_element_type=jnp.float32
        )
        grad_scores = (probs * (grad_probs - delta[:, :, None])).astype(jnp.bfloat16)
        grad_query = (
            grad_query
            + jnp.einsum("hqk,khd->qhd", grad_scores, key_block, preferred_element_type=jnp.float32)
            * score_scale
        )
        key_term = (
            jnp.einsum("hqk,qhd->khd", grad_scores, query_heads, preferred_element_type=jnp.float32)
            * score_scale
        )
        value_term = jnp.einsum(
            "hqk,qhd->khd",
            probs.astype(jnp.bfloat16),
            grad_heads,
            preferred_element_type=jnp.float32,
        )
        grad_key = lax.dynamic_update_slice_in_dim(
            grad_key, key_term.reshape(attend_block_rows, D), offset, 0
        )
        grad_value = lax.dynamic_update_slice_in_dim(
            grad_value, value_term.reshape(attend_block_rows, D), offset, 0
        )
        return (grad_query, grad_key, grad_value)

    grad_query, grad_key_all, grad_value_all = lax.fori_loop(
        0, amount // attend_block_rows, one_block, back_state
    )
    grad_key, grad_value = (
        lax.psum_scatter(
            grad_key_all.astype(jnp.bfloat16), "ctx", scatter_dimension=0, tiled=True
        ).astype(jnp.float32),
        lax.psum_scatter(
            grad_value_all.astype(jnp.bfloat16), "ctx", scatter_dimension=0, tiled=True
        ).astype(jnp.float32),
    )
    grad_query = grad_query.reshape(row_count, D)
    grad_inputs, grad_qkv_t, grad_query_b, grad_value_b = head_backward(
        inputs, grad_first, grad_query, grad_key, grad_value, params[0]
    )
    matrix, vectors = pack_grads(grad_qkv_t, grad_query_b, grad_value_b, tail_grads)
    vector_total = lax.psum(vectors, ("ctx", "fsdp"))
    new_vectors, new_vfirst, new_vsecond = adam_update(
        vector_rows, vector_total, vector_first, vector_second
    )
    grads = lax.psum_scatter(matrix.astype(jnp.bfloat16), "fsdp", scatter_dimension=0, tiled=True)
    grad_out = lax.psum(grads, "ctx").astype(jnp.float32)
    weights_out, first_out, second_out = adam_update(weight_rows, grad_out, first_rows, second_rows)
    return (
        output.reshape(1, row_count, D),
        grad_inputs.reshape(1, row_count, D),
        grad_out,
        weights_out,
        first_out,
        second_out,
        vector_total,
        new_vectors,
        new_vfirst,
        new_vsecond,
    )


def solution(mesh):
    return jax.shard_map(
        local,
        mesh=mesh,
        in_specs=(
            P("fsdp", "ctx", None),
            P("fsdp", "ctx", None),
            P("fsdp", None),
            P("fsdp", None),
            P("fsdp", None),
            P(),
            P(),
            P(),
        ),
        out_specs=(
            P("fsdp", "ctx", None),
            P("fsdp", "ctx", None),
            P("fsdp", None),
            P("fsdp", None),
            P("fsdp", None),
            P("fsdp", None),
            P(),
            P(),
            P(),
            P(),
        ),
        check_vma=False,
    )
```

profile of v0, /device:TPU:0, one launch (start us, length us, event | category | flops | bytes accessed | tf_op | source)
XLA Modules:
  0.0 671.2 jit_solution(5482531895368750081)
XLA Ops:
  7.2 0.0 all-gather.4.cloned.1.call-start
  7.2 5.0 convert_element_type.122
  12.2 0.0 all-gather.4.cloned.1.call-update
  12.2 0.0 all-gather.6.cloned.1.call-start
  12.3 128.0 %all-gather.4.cloned.1.call-done = bf16[12288,1024]{1,0:T(8,128)(2,1)} async-done(((bf16[1536,1024]{1,0:T(8,128)(2,1)}), bf16[12288,1024]{1,0:T(8,128)(2,1)}) %all-gather.4.cloned.1.call-update) | async-done | bytes 25165840 | tf_op jit(solution)/shard_map/all_gather | solution.py:196
  140.3 5.0 fusion.11
  145.2 0.7 slice.133
  146.0 0.0 all-gather.8.cloned.1.call-start
  146.1 0.8 fusion.89
  147.0 0.0 reduce-scatter.12.cloned.1.call-start
  147.0 0.2 copy.29
  147.2 26.9 %all-gather.6.cloned.1.call-done = bf16[512,1024]{1,0:T(8,128)(2,1)} async-done(((bf16[128,1024]{1,0:T(8,128)(2,1)}), bf16[512,1024]{1,0:T(8,128)(2,1)}) %all-gather.6.cloned.1.call-update) | async-done | bytes 1048592 | tf_op jit(solution)/shard_map/all_gather | solution.py:205
  174.1 1.5 copy.30
  175.6 0.8 multiply_reduce_fusion
  176.5 1.2 fusion.19
  177.7 0.8 copy-done
  178.5 25.2 %all-gather.8.cloned.1.call-done = bf16[512,1024]{1,0:T(8,128)(2,1)} async-done(((bf16[128,1024]{1,0:T(8,128)(2,1)}), bf16[512,1024]{1,0:T(8,128)(2,1)}) %all-gather.8.cloned.1.call-update) | async-done | bytes 1048592 | tf_op jit(solution)/shard_map/all_gather | solution.py:206
  203.7 1.5 copy.31
  205.2 5.7 fusion.78
  210.9 2.6 fusion.114
  213.5 0.2 multiply_reduce_fusion.5
  213.8 9.7 %fusion.25 = (bf16[128,4096]{1,0:T(8,128)(2,1)S(1)}, f32[128,4096]{1,0:T(8,128)S(1)}) fusion(f32[4096]{0:T(1024)S(1)} %bitcast.132, bf16[12288,1024]{1,0:T(8,128)(2,1)} %all-gather.4.cloned.1.call-done, f32[128,1024]{1,0:T(8,128)S(1)} %get-tuple-element.103, f32[1024]{0:T(1024)S(1)} %bitcast.121, f32[1024]{0:T(1024)S(1)} %bitcast.113, ...), kind=kOutput, calls=%fused_computation.34 | convolution fusion | flops 1109000192 | bytes 12084224 | tf_op jit(solution)/shard_map/dot_general | solution.py:19
  223.4 5.3 fusion.115
  228.7 0.2 multiply_reduce_fusion.4
  229.0 0.3 fusion.87
  229.3 1.0 fusion.109
  230.2 6.7 fusion.116
  236.9 5.3 multiply_reduce_fusion.1
  242.2 0.2 fusion.111
  242.5 0.8 copy-done.14
  243.2 2.0 fusion.74
  245.3 0.2 copy.32
  245.5 3.2 fusion.47
  248.7 1.3 copy.35
  250.0 0.0 reduce-scatter.12.cloned.1.call-update
  250.0 0.0 reduce-scatter.10.cloned.1.call-start
  250.1 0.1 multiply_reduce_fusion.2
  250.2 3.9 multiply_convert_fusion
  254.1 1.4 multiply_convert_fusion.1
  255.5 2.3 copy.33
  257.8 0.0 reduce-scatter.10.cloned.1.call-update
  257.8 0.2 reduce-scatter.8.cloned.1.call-start
  258.1 3.1 convolution_convert_fusion.3
  261.2 1.5 fusion.113
  262.7 5.6 convolution_convert_fusion
  268.3 5.6 convolution_convert_fusion.1
  273.9 2.9 reduce-scatter.12.cloned.1.call-done
  276.8 1.1 copy.36
  278.0 27.4 %reduce-scatter.10.cloned.1.call-done = bf16[128,1024]{1,0:T(8,128)(2,1)} async-done(((bf16[512,1024]{1,0:T(8,128)(2,1)}), bf16[128,1024]{1,0:T(8,128)(2,1)}) %reduce-scatter.10.cloned.1.call-update) | async-done | bytes 262160
  305.4 1.8 copy.34
  307.2 2.9 convolution_convert_fusion.2
  310.1 59.3 %pad_maximum_fusion = bf16[12288,1024]{1,0:T(8,128)(2,1)} fusion(bf16[4096,1024]{1,0:T(8,128)(2,1)} %convolution_convert_fusion, bf16[4096,1024]{1,0:T(8,128)(2,1)} %convolution_convert_fusion.1, bf16[1024,1024]{1,0:T(8,128)(2,1)} %convolution_convert_fusion.3, bf16[3072,1024]{1,0:T(8,128)(2,1)S(1)} %convolution_convert_fusion.2), kind=kLoop, calls=%fused_computation | loop fusion | flops 100663296 | bytes 50331648 | tf_op jit(solution)/shard_map/concatenate | solution.py:148
  369.4 0.0 all-reduce.2.cloned.1.call-start
  369.5 154.8 %reduce-scatter.8.cloned.1.call-done = bf16[1536,1024]{1,0:T(8,128)(2,1)} async-done(((bf16[12288,1024]{1,0:T(8,128)(2,1)}), bf16[1536,1024]{1,0:T(8,128)(2,1)}) %reduce-scatter.8.cloned.1.call-update) | async-done | bytes 3145744 | tf_op jit(solution)/shard_map/reduce_scatter | solution.py:317
  524.3 0.0 all-reduce.2.cloned.1.call-update
  524.4 0.1 convert_reduce_fusion
  524.5 0.1 stack.24
  524.5 0.1 convert_reduce_fusion.1
  524.7 0.1 concatenate.13
  524.8 43.9 %psum.15 = f32[12,1024]{1,0:T(8,128)S(1)} all-reduce(f32[12,1024]{1,0:T(8,128)S(1)} %concatenate.13), channel_id=1, replica_groups=mesh['ctx'=4,'fsdp'=8] {'ctx','fsdp'}, use_global_device_ids=true, to_apply=%region_24.0 | all-reduce | flops 12288 | bytes 98304 | tf_op jit(solution)/shard_map/psum | solution.py:313
  568.7 0.7 multiply_subtract_fusion.1
  569.4 4.6 fusion.71
  574.0 74.7 %all-reduce.2.cloned.1.call-done = bf16[1536,1024]{1,0:T(8,128)(2,1)} async-done(((bf16[1536,1024]{1,0:T(8,128)(2,1)}), bf16[1536,1024]{1,0:T(8,128)(2,1)}) %all-reduce.2.cloned.1.call-update) | async-done | bytes 3145744 | tf_op jit(solution)/shard_map/psum | solution.py:318
  648.8 15.3 %multiply_subtract_fusion = (f32[1536,1024]{1,0:T(8,128)}, f32[1536,1024]{1,0:T(8,128)}, f32[1536,1024]{1,0:T(8,128)}, f32[1536,1024]{1,0:T(8,128)}) fusion(f32[1536,1024]{1,0:T(8,128)} %param.10, f32[1536,1024]{1,0:T(8,128)} %param.11, f32[1536,1024]{1,0:T(8,128)} %param.12, bf16[1536,1024]{1,0:T(8,128)(2,1)} %all-reduce.2.cloned.1.call-done), kind=kLoop, calls=%fused_computation.13 | loop fusion | flops 25165824 | bytes 47185920 | tf_op jit(solution)/shard_map/sub | solution.py:170
  (65 shorter events, 0.3 us)
Async XLA Ops:
  7.2 133.1 %all-gather.4.cloned.1.call-start = ((), (), s32[]{:S(2)}) async-start(), calls=%async_computation.3 | async-start | bytes 28311552 | tf_op jit(solution)/shard_map/all_gather | solution.py:196
  12.2 128.1 %copy-start.20 = (bf16[1,128,1024]{2,1,0:T(8,128)(2,1)S(1)}, bf16[1,128,1024]{2,1,0:T(8,128)(2,1)}, u32[]{:S(2)}) copy-start(bf16[1,128,1024]{2,1,0:T(8,128)(2,1)} %param.8) | copy-start | bytes 786436
  12.2 133.9 %copy-start.21 = (f32[12,1024]{1,0:T(8,128)S(1)}, f32[12,1024]{1,0:T(8,128)}, u32[]{:S(2)}) copy-start(f32[12,1024]{1,0:T(8,128)} %param.13) | copy-start | bytes 147460
  12.2 161.9 %all-gather.6.cloned.1.call-start = ((), (), s32[]{:S(2)}) async-start(), calls=%async_computation.4 | async-start | bytes 1310720 | tf_op jit(solution)/shard_map/all_gather | solution.py:205
  146.0 57.7 %all-gather.8.cloned.1.call-start = ((), (), s32[]{:S(2)}) async-start(), calls=%async_computation.5 | async-start | bytes 1310720 | tf_op jit(solution)/shard_map/all_gather | solution.py:206
  147.0 129.9 %reduce-scatter.12.cloned.1.call-start = ((), (), s32[]{:S(2)}) async-start(), calls=%async_computation.9 | async-start | bytes 1310720
  147.2 29.3 %copy-start.10 = (bf16[128,1024]{0,1:T(8,128)(2,1)}, bf16[128,1024]{0,1:T(8,128)(2,1)S(1)}, u32[]{:S(2)}) copy-start(bf16[128,1024]{0,1:T(8,128)(2,1)S(1)} %copy.29) | copy-start | bytes 786436
  176.5 2.0 copy-start
  205.2 5.7 copy-start.3
  210.9 39.2 %copy-start.18 = (bf16[128,16,64]{0,2,1:T(8,128)(2,1)}, bf16[128,16,64]{0,2,1:T(8,128)(2,1)S(1)}, u32[]{:S(2)}) copy-start(bf16[128,16,64]{0,2,1:T(8,128)(2,1)S(1)} %fusion.78) | copy-start | bytes 786436
  213.5 28.7 %copy-start.1 = (f32[128,1024]{1,0:T(8,128)}, f32[128,1024]{1,0:T(8,128)S(1)}, u32[]{:S(2)}) copy-start(f32[128,1024]{1,0:T(8,128)S(1)} %get-tuple-element.103) | copy-start | bytes 1572868
  223.4 5.3 copy-start.4
  223.4 5.5 copy-start.8
  230.2 6.7 copy-start.12
  236.9 5.3 copy-start.6
  242.4 0.8 copy-start.14
  250.0 55.4 %reduce-scatter.10.cloned.1.call-start = ((), (), s32[]{:S(2)}) async-start(), calls=%async_computation.8 | async-start | bytes 1310720
  250.2 3.9 copy-start.11
  255.5 2.6 copy-start.19
  257.8 266.5 %reduce-scatter.8.cloned.1.call-start = ((), (), s32[]{:S(2)}) async-start(), calls=%async_computation.6 | async-start | bytes 28311552 | tf_op jit(solution)/shard_map/reduce_scatter | solution.py:317
  261.2 1.5 copy-start.5
  261.2 1.5 copy-start.13
  262.7 5.6 copy-start.2
  262.7 5.6 copy-start.7
  369.4 155.0 %copy-start.9 = (bf16[1,128,1024]{2,1,0:T(8,128)(2,1)S(1)}, bf16[1,128,1024]{2,1,0:T(8,128)(2,1)}, u32[]{:S(2)}) copy-start(bf16[1,128,1024]{2,1,0:T(8,128)(2,1)} %param.9) | copy-start | bytes 786436
  369.4 199.3 %copy-start.23 = (f32[12,1024]{1,0:T(8,128)S(1)}, f32[12,1024]{1,0:T(8,128)}, u32[]{:S(2)}) copy-start(f32[12,1024]{1,0:T(8,128)} %param.14) | copy-start | bytes 147460
  369.4 199.3 %copy-start.24 = (f32[12,1024]{1,0:T(8,128)S(1)}, f32[12,1024]{1,0:T(8,128)}, u32[]{:S(2)}) copy-start(f32[12,1024]{1,0:T(8,128)} %param.15) | copy-start | bytes 147460
  369.4 279.3 %all-reduce.2.cloned.1.call-start = ((), (), s32[]{:S(2)}) async-start(), calls=%async_computation.7 | async-start | bytes 6291456 | tf_op jit(solution)/shard_map/psum | solution.py:318
  524.3 45.1 %copy-start.15 = (f32[128,1024]{1,0:T(8,128)S(1)}, f32[128,1024]{1,0:T(8,128)}, u32[]{:S(2)}) copy-start(f32[128,1024]{1,0:T(8,128)} %copy-done.14) | copy-start | bytes 1572868
  524.3 45.1 %copy-start.16 = (bf16[128,1024]{0,1:T(8,128)(2,1)S(1)}, bf16[128,1024]{0,1:T(8,128)(2,1)}, u32[]{:S(2)}) copy-start(bf16[128,1024]{0,1:T(8,128)(2,1)} %copy.34) | copy-start | bytes 786436
  524.3 45.1 %copy-start.17 = (bf16[128,16,64]{0,2,1:T(8,128)(2,1)S(1)}, bf16[128,16,64]{0,2,1:T(8,128)(2,1)}, u32[]{:S(2)}) copy-start(bf16[128,16,64]{0,2,1:T(8,128)(2,1)} %get-tuple-element.89) | copy-start | bytes 786436
  568.7 5.3 copy-start.22
Sparse Core Ops, SparseCore 0:
  12.3 127.9 all-gather.3
  146.1 27.9 all-gather.5
  176.3 27.3 all-gather.7
  250.1 26.6 reduce-scatter.11
  279.6 25.7 reduce-scatter.9
  369.5 154.7 reduce-scatter.7
  526.7 122.0 all-reduce.1
where the time goes:
time: 679 us; the launch traced here: 671 us
  waiting for transfers between devices  440 us (65%)
  other arithmetic  84.5 us (12%)
  matrix products  74.8 us (11%)
  blocking collectives  43.9 us (6%)
  between operations  14.8 us (2%)
  local copies, waits for them, and re-layouts  12.4 us (2%)
    reduce_scatter x1, waiting for transfers between devices, local(): lax.psum_scatter(matrix.astype(jnp.bfloat16), 'fsdp', scatter_dimension=0...  155 us
    all_gather x1, waiting for transfers between devices, local(): lax.all_gather(weight_rows.astype(jnp.bfloat16), 'fsdp', axis=0, tiled=True)  128 us
    psum x1, waiting for transfers between devices, local(): grad_out = lax.psum(grads, 'ctx').astype(jnp.float32)  74.7 us
    concatenate x1, other arithmetic, pack_grads(): jnp.concatenate([grad_qkv_t, tail_grads[0], tail_grads[4], tail_grads[6]]...  59.3 us
    psum x1, blocking collectives, local(): vector_total = lax.psum(vectors, ('ctx', 'fsdp'))  43.9 us
    unnamed x9, waiting for transfers between devices  30.5 us
    all_gather x1, waiting for transfers between devices, local(): key_piece = lax.all_gather(key_rows, 'ctx', axis=0, tiled=True)  26.9 us
    all_gather x1, waiting for transfers between devices, local(): value_piece = lax.all_gather(value_rows, 'ctx', axis=0, tiled=True)  25.2 us
  transfers between devices with their start and end apart: 7, of which 7 were waited for; matrix products, arithmetic and copies ran while one was open for 5% of the time, Pallas kernels for 0%

commit v1 on v0

--- a/solution.py
+++ b/solution.py
@@ -13,6 +13,28 @@
 adam_eps = 1e-08
 norm_eps = 1e-05
 adam_step = 2
+
+
+def laid_out(tiles, dim):
+    tiles = jnp.moveaxis(tiles, 0, dim)
+    shape = tiles.shape
+    return tiles.reshape(*shape[:dim], shape[dim] * shape[dim + 1], *shape[dim + 2 :])
+
+
+def collected_by_bits(value, axis):
+    peers = lax.axis_size(axis)
+    blocks = value[None]
+    for level in range(peers.bit_length() - 1):
+        distance = 1 << level
+        received = lax.ppermute(blocks, axis, [(i, i ^ distance) for i in range(peers)])
+        both = jnp.stack([blocks, received])
+        upper = lax.axis_index(axis) >> level & 1
+        blocks = jnp.where(upper == 0, both, both[::-1]).reshape(-1, *value.shape)
+    return blocks
+
+
+def collect(x, axis, dim):
+    return laid_out(collected_by_bits(x, axis), dim)
 
 
 def mat_nt(left, right):
@@ -193,7 +215,7 @@
     head_width = D // HEADS
     score_scale = 1.0 / math.sqrt(head_width)
     vectors_b = vector_rows.astype(jnp.bfloat16)
-    gathered = lax.all_gather(weight_rows.astype(jnp.bfloat16), "fsdp", axis=0, tiled=True)
+    gathered = collect(weight_rows.astype(jnp.bfloat16), "fsdp", 0)
     params = unpack(gathered, vectors_b)
     query_rows, key_rows, value_rows = project(inputs, params)
     query_heads = split_heads(query_rows)

time: 679 us -> 1020 us (1.50)
  waiting for transfers between devices: 440 us -> 723 us
  other arithmetic: 84.5 us -> 140 us
    ppermute x0 -> x3, waiting for transfers between devices: none -> 412 us  [collected_by_bits(): lax.ppermute(blocks, axis, [(i, i ^ distance) for i in range(peers)])]
    all_gather x1 -> x0, waiting for transfers between devices: 128 us -> none  [local(): lax.all_gather(weight_rows.astype(jnp.bfloat16), 'fsdp', axis=0, tiled=True)]
    another operation x0 -> x5, other arithmetic: none -> 35 us  [collected_by_bits(): both = jnp.stack([blocks, received])]
    select_n x0 -> x2, other arithmetic: none -> 23.2 us  [collected_by_bits(): blocks = jnp.where(upper == 0, both, both[::-1]).reshape(-1, *value.shape)]
    unnamed x9 -> x8, waiting for transfers between devices: 30.5 us -> 28 us
  transfers between devices with their start and end apart: 7 -> 9, of which waited for: 7 -> 9; matrix products, arithmetic and copies ran while one was open for 5% -> 4% of each run, Pallas kernels for 0% -> 0%
where the time goes in v1:
time: 1020 us; the launch traced here: 1010 us
  waiting for transfers between devices  723 us (71%)
  other arithmetic  140 us (14%)
  matrix products  71.1 us (7%)
  blocking collectives  43.6 us (4%)
  between operations  15.2 us (1%)
  local copies, waits for them, and re-layouts  13.8 us (1%)
    ppermute x3, waiting for transfers between devices, collected_by_bits(): lax.ppermute(blocks, axis, [(i, i ^ distance) for i in range(peers)])  412 us
    reduce_scatter x1, waiting for transfers between devices, local(): lax.psum_scatter(matrix.astype(jnp.bfloat16), 'fsdp', scatter_dimension=0...  155 us
    psum x1, waiting for transfers between devices, local(): grad_out = lax.psum(grads, 'ctx').astype(jnp.float32)  74.7 us
    concatenate x1, other arithmetic, pack_grads(): jnp.concatenate([grad_qkv_t, tail_grads[0], tail_grads[4], tail_grads[6]]...  59.3 us
    psum x1, blocking collectives, local(): vector_total = lax.psum(vectors, ('ctx', 'fsdp'))  43.6 us
    another operation x5, other arithmetic, collected_by_bits(): both = jnp.stack([blocks, received])  35 us
    all_gather x1, waiting for transfers between devices, local(): key_piece = lax.all_gather(key_rows, 'ctx', axis=0, tiled=True)  28.4 us
    unnamed x8, waiting for transfers between devices  28 us
  transfers between devices with their start and end apart: 9, of which 9 were waited for; matrix products, arithmetic and copies ran while one was open for 4% of the time, Pallas kernels for 0%

profile of v1, /device:TPU:0, one launch (start us, length us, event | category | flops | bytes accessed | tf_op | source)
XLA Modules:
  0.0 1012.7 jit_solution(9006029182413581609)
XLA Ops:
  7.2 6.4 convert_bitcast_fusion.1
  13.6 0.5 collective-permute-start
  14.1 5.5 collective-permute-done
  19.6 1.7 copy-done.1
  21.3 3.4 pad_maximum_fusion.3
  24.7 7.3 fusion.20
  31.9 2.8 collective-permute-start.1
  34.8 136.1 %collective-permute-done.1 = bf16[2,1536,1024]{2,1,0:T(8,128)(2,1)} collective-permute-done((bf16[2,1536,1024]{2,1,0:T(8,128)(2,1)}, bf16[2,1536,1024]{2,1,0:T(8,128)(2,1)}, u32[]{:S(2)}, u32[]{:S(2)}) %collective-permute-start.1) | collective-permute-done | bytes 6291488 | tf_op jit(solution)/shard_map/ppermute | solution.py:29
  170.9 6.1 pad_maximum_fusion.2
  177.0 8.1 reverse_select_fusion.1
  185.1 1.8 collective-permute-start.2
  186.9 270.3 %collective-permute-done.2 = bf16[4,1536,1024]{2,1,0:T(8,128)(2,1)} collective-permute-done((bf16[4,1536,1024]{2,1,0:T(8,128)(2,1)}, bf16[4,1536,1024]{2,1,0:T(8,128)(2,1)}, u32[]{:S(2)}, u32[]{:S(2)}) %collective-permute-start.2) | collective-permute-done | bytes 12582944 | tf_op jit(solution)/shard_map/ppermute | solution.py:29
  457.2 11.8 %pad_maximum_fusion = bf16[2,4,1536,1024]{3,2,1,0:T(8,128)(2,1)S(1)} fusion(bf16[1,4,1536,1024]{3,2,1,0:T(8,128)(2,1)} %bitcast.9, bf16[1,4,1536,1024]{3,2,1,0:T(8,128)(2,1)} %bitcast.7), kind=kLoop, calls=%fused_computation.1 | loop fusion | flops 12582912 | bytes 50331648 | tf_op jit(solution)/shard_map/stack | solution.py:30
  469.0 15.2 %reverse_select_fusion = bf16[2,4,1536,1024]{3,2,1,0:T(8,128)(2,1)} fusion(bf16[2,4,1536,1024]{3,2,1,0:T(8,128)(2,1)S(1)} %pad_maximum_fusion, pred[]{:T(512)S(6)} %eq.9), kind=kLoop, calls=%fused_computation | loop fusion | flops 12582912 | bytes 50331648 | tf_op jit(solution)/shard_map/jit(_where)/select_n | solution.py:32
  484.2 4.6 fusion.21
  488.8 0.7 slice.135
  489.7 0.6 slice_convert_fusion.2
  490.3 1.0 fusion.94
  491.3 0.6 reduce-scatter.12.cloned.1.call-start
  491.9 0.6 copy.26
  492.5 28.4 %all-gather.3.cloned.1.call-done = bf16[512,1024]{0,1:T(8,128)(2,1)} async-done(((bf16[128,1024]{0,1:T(8,128)(2,1)}), bf16[512,1024]{0,1:T(8,128)(2,1)}) %all-gather.3.cloned.1.call-update) | async-done | bytes 1048592 | tf_op jit(solution)/shard_map/all_gather | solution.py:227
  520.9 2.1 multiply_reduce_fusion
  523.0 2.0 copy-done
  525.0 1.2 fusion.24
  526.2 25.0 %all-gather.5.cloned.1.call-done = bf16[512,1024]{0,1:T(8,128)(2,1)} async-done(((bf16[128,1024]{0,1:T(8,128)(2,1)}), bf16[512,1024]{0,1:T(8,128)(2,1)}) %all-gather.5.cloned.1.call-update) | async-done | bytes 1048592 | tf_op jit(solution)/shard_map/all_gather | solution.py:228
  551.3 5.6 fusion.83
  557.0 2.7 fusion.119
  559.6 0.2 multiply_reduce_fusion.5
  559.9 10.8 %fusion.30 = (bf16[128,4096]{1,0:T(8,128)(2,1)S(1)}, f32[128,4096]{1,0:T(8,128)}) fusion(f32[4096]{0:T(1024)S(1)} %bitcast.159, bf16[12288,1024]{1,0:T(8,128)(2,1)} %bitcast.117, f32[128,1024]{1,0:T(8,128)S(1)} %get-tuple-element.107, f32[1024]{0:T(1024)S(1)} %bitcast.148, f32[1024]{0:T(1024)S(1)} %bitcast.140, f32[128]{0:T(128)S(1)} %add_rsqrt_fusion.1, ...), kind=kOutput, calls=%fused_computation.43 | convolution fusion | flops 1109000192 | bytes 12084224 | tf_op jit(solution)/shard_map/dot_general | solution.py:41
  570.9 1.4 fusion.120
  572.4 0.2 multiply_reduce_fusion.4
  572.6 0.8 fusion.92
  573.4 1.7 fusion.114
  575.1 6.0 fusion.121
  581.1 3.5 multiply_reduce_fusion.1
  584.6 0.2 fusion.116
  584.8 0.8 copy-done.10
  585.6 1.2 fusion.79
  586.8 1.1 copy.19
  587.9 3.2 fusion.52
  591.2 1.3 copy.22
  592.6 0.1 multiply_reduce_fusion.2
  592.7 3.8 multiply_convert_fusion
  596.5 1.4 multiply_convert_fusion.1
  597.9 2.3 copy.20
  600.2 0.3 reduce-scatter.8.cloned.1.call-start
  600.5 3.2 convolution_convert_fusion.3
  603.7 2.8 fusion.118
  606.5 5.6 convolution_convert_fusion
  612.1 5.7 convolution_convert_fusion.1
  617.8 0.5 reduce-scatter.12.cloned.1.call-done
  618.2 1.1 copy.23
  619.4 27.4 %reduce-scatter.10.cloned.1.call-done = bf16[128,1024]{1,0:T(8,128)(2,1)} async-done(((bf16[512,1024]{1,0:T(8,128)(2,1)}), bf16[128,1024]{1,0:T(8,128)(2,1)}) %reduce-scatter.10.cloned.1.call-update) | async-done | bytes 262160
  646.8 1.8 copy.21
  648.6 2.9 convolution_convert_fusion.2
  651.5 59.3 %pad_maximum_fusion.1 = bf16[12288,1024]{1,0:T(8,128)(2,1)} fusion(bf16[4096,1024]{1,0:T(8,128)(2,1)} %convolution_convert_fusion, bf16[4096,1024]{1,0:T(8,128)(2,1)} %convolution_convert_fusion.1, bf16[1024,1024]{1,0:T(8,128)(2,1)} %convolution_convert_fusion.3, bf16[3072,1024]{1,0:T(8,128)(2,1)S(1)} %convolution_convert_fusion.2), kind=kLoop, calls=%fused_computation.2 | loop fusion | flops 100663296 | bytes 50331648 | tf_op jit(solution)/shard_map/concatenate | solution.py:170
  711.0 154.9 %reduce-scatter.8.cloned.1.call-done = bf16[1536,1024]{1,0:T(8,128)(2,1)} async-done(((bf16[12288,1024]{1,0:T(8,128)(2,1)}), bf16[1536,1024]{1,0:T(8,128)(2,1)}) %reduce-scatter.8.cloned.1.call-update) | async-done | bytes 3145744 | tf_op jit(solution)/shard_map/reduce_scatter | solution.py:339
  866.1 0.1 convert_reduce_fusion.1
  866.3 0.1 concatenate.13
  866.3 43.6 %psum.15 = f32[12,1024]{1,0:T(8,128)S(1)} all-reduce(f32[12,1024]{1,0:T(8,128)S(1)} %concatenate.13), channel_id=1, replica_groups=mesh['ctx'=4,'fsdp'=8] {'ctx','fsdp'}, use_global_device_ids=true, to_apply=%region_24.25 | all-reduce | flops 12288 | bytes 98304 | tf_op jit(solution)/shard_map/psum | solution.py:335
  910.0 0.7 multiply_subtract_fusion.1
  910.7 4.6 fusion.76
  915.4 74.7 %all-reduce.2.cloned.1.call-done = bf16[1536,1024]{1,0:T(8,128)(2,1)} async-done(((bf16[1536,1024]{1,0:T(8,128)(2,1)}), bf16[1536,1024]{1,0:T(8,128)(2,1)}) %all-reduce.2.cloned.1.call-update) | async-done | bytes 3145744 | tf_op jit(solution)/shard_map/psum | solution.py:340
  990.1 15.3 %multiply_subtract_fusion = (f32[1536,1024]{1,0:T(8,128)}, f32[1536,1024]{1,0:T(8,128)}, f32[1536,1024]{1,0:T(8,128)}, f32[1536,1024]{1,0:T(8,128)}) fusion(f32[1536,1024]{1,0:T(8,128)} %param.10, f32[1536,1024]{1,0:T(8,128)} %param.11, f32[1536,1024]{1,0:T(8,128)} %param.12, bf16[1536,1024]{1,0:T(8,128)(2,1)} %all-reduce.2.cloned.1.call-done), kind=kLoop, calls=%fused_computation.19 | loop fusion | flops 25165824 | bytes 47185920 | tf_op jit(solution)/shard_map/sub | solution.py:192
  (110 shorter events, 0.7 us)
Async XLA Ops:
  7.2 513.7 %all-gather.3.cloned.1.call-start = ((), (), s32[]{:S(2)}) async-start(), calls=%async_computation.3 | async-start | bytes 1310720 | tf_op jit(solution)/shard_map/all_gather | solution.py:227
  13.6 6.0 collective-permute-start
  19.6 1.7 copy-start.1
  31.9 139.0 %collective-permute-start.1 = (bf16[2,1536,1024]{2,1,0:T(8,128)(2,1)}, bf16[2,1536,1024]{2,1,0:T(8,128)(2,1)}, u32[]{:S(2)}, u32[]{:S(2)}) collective-permute-start(bf16[2,1536,1024]{2,1,0:T(8,128)(2,1)} %get-tuple-element.86), channel_id=1, source_target_pairs={{0,2},{1,3},{2,0},{3,1},{4,6},{5,7},{6,4},{7,5},{8,10},{9,11},{10,... | collective-permute-start | bytes 18874376 | tf_op jit(solution)/shard_map/ppermute | solution.py:29
  185.1 272.1 %collective-permute-start.2 = (bf16[4,1536,1024]{2,1,0:T(8,128)(2,1)}, bf16[4,1536,1024]{2,1,0:T(8,128)(2,1)}, u32[]{:S(2)}, u32[]{:S(2)}) collective-permute-start(bf16[4,1536,1024]{2,1,0:T(8,128)(2,1)} %bitcast.8), channel_id=1, source_target_pairs={{0,4},{1,5},{2,6},{3,7},{4,0},{5,1},{6,2},{7,3},{8,12},{9,13},{10,... | collective-permute-start | bytes 37748744 | tf_op jit(solution)/shard_map/ppermute | solution.py:29
  469.0 15.2 %copy-start.16 = (bf16[1,128,1024]{2,1,0:T(8,128)(2,1)S(1)}, bf16[1,128,1024]{2,1,0:T(8,128)(2,1)}, u32[]{:S(2)}) copy-start(bf16[1,128,1024]{2,1,0:T(8,128)(2,1)} %param.8) | copy-start | bytes 786436
  484.2 5.4 copy-start.17
  489.6 61.7 %all-gather.5.cloned.1.call-start = ((), (), s32[]{:S(2)}) async-start(), calls=%async_computation.4 | async-start | bytes 1310720 | tf_op jit(solution)/shard_map/all_gather | solution.py:228
  491.3 34.9 %copy-start.7 = (bf16[128,1024]{0,1:T(8,128)(2,1)}, bf16[128,1024]{0,1:T(8,128)(2,1)S(1)}, u32[]{:S(2)}) copy-start(bf16[128,1024]{0,1:T(8,128)(2,1)S(1)} %get-tuple-element.89) | copy-start | bytes 786436
  491.3 126.9 %reduce-scatter.12.cloned.1.call-start = ((), (), s32[]{:S(2)}) async-start(), calls=%async_computation.8 | async-start | bytes 1310720
  523.0 2.0 copy-start
  551.3 8.6 copy-start.21
  551.3 8.6 copy-start.27
  556.9 2.9 copy-start.14
  556.9 13.9 %slice-start = ((s8[25165824]{0:T(1024)(128)(4,1)}), s8[4194304]{0:T(1024)(128)(4,1)S(1)}, s32[]{:S(2)}) async-start(s8[25165824]{0:T(1024)(128)(4,1)} %bitcast.119), calls=%async_computation.9 | async-start | bytes 8388608
  559.6 11.2 %copy-start.28 = (f32[128]{0:T(128)}, f32[128]{0:T(128)S(1)}, u32[]{:S(2)}) copy-start(f32[128]{0:T(128)S(1)} %broadcast_multiply_fusion.5) | copy-start | bytes 1540
  559.8 11.0 %copy-start.35 = (f32[128]{0:T(128)}, f32[128]{0:T(128)S(1)}, u32[]{:S(2)}) copy-start(f32[128]{0:T(128)S(1)} %add_rsqrt_fusion.1) | copy-start | bytes 1540
  559.9 10.9 %slice-start.1 = ((s8[25165824]{0:T(1024)(128)(4,1)}), s8[4194304]{0:T(1024)(128)(4,1)S(1)}, s32[]{:S(2)}) async-start(s8[25165824]{0:T(1024)(128)(4,1)} %bitcast.119), calls=%async_computation.10 | async-start | bytes 8388608
  559.9 10.9 %slice-start.2 = ((s8[25165824]{0:T(1024)(128)(4,1)}), s8[4194304]{0:T(1024)(128)(4,1)S(1)}, s32[]{:S(2)}) async-start(s8[25165824]{0:T(1024)(128)(4,1)} %bitcast.119), calls=%async_computation.11 | async-start | bytes 8388608
  559.9 10.9 %slice-start.3 = ((s8[25165824]{0:T(1024)(128)(4,1)}), s8[4194304]{0:T(1024)(128)(4,1)S(1)}, s32[]{:S(2)}) async-start(s8[25165824]{0:T(1024)(128)(4,1)} %bitcast.119), calls=%async_computation.12 | async-start | bytes 8388608
  559.9 10.9 %slice-start.4 = ((s8[25165824]{0:T(1024)(128)(4,1)}), s8[4194304]{0:T(1024)(128)(4,1)S(1)}, s32[]{:S(2)}) async-start(s8[25165824]{0:T(1024)(128)(4,1)} %bitcast.119), calls=%async_computation.13 | async-start | bytes 8388608
  559.9 10.9 %slice-start.5 = ((s8[25165824]{0:T(1024)(128)(4,1)}), s8[4194304]{0:T(1024)(128)(4,1)S(1)}, s32[]{:S(2)}) async-start(s8[25165824]{0:T(1024)(128)(4,1)} %bitcast.119), calls=%async_computation.14 | async-start | bytes 8388608
  559.9 10.9 %copy-start.34 = (f32[1,1024]{1,0:T(1,128)S(1)}, f32[1,1024]{1,0:T(1,128)}, u32[]{:S(2)}) copy-start(f32[1,1024]{1,0:T(1,128)} %get-tuple-element.96) | copy-start | bytes 12292
  570.8 1.6 copy-start.2
  570.9 1.7 copy-start.5
  570.9 2.5 copy-start.25
  575.1 6.0 copy-start.29
  581.1 3.5 copy-start.30
  581.1 3.5 copy-start.36
  584.8 0.8 copy-start.10
  587.9 4.7 copy-start.15
  592.5 4.0 copy-start.8
  592.5 54.3 %reduce-scatter.10.cloned.1.call-start = ((), (), s32[]{:S(2)}) async-start(), calls=%async_computation.7 | async-start | bytes 1310720
  600.2 6.3 copy-start.9
  600.2 265.6 %reduce-scatter.8.cloned.1.call-start = ((), (), s32[]{:S(2)}) async-start(), calls=%async_computation.5 | async-start | bytes 28311552 | tf_op jit(solution)/shard_map/reduce_scatter | solution.py:339
  600.5 6.0 copy-start.3
  606.5 5.6 copy-start.4
  606.5 5.6 copy-start.22
  606.5 5.6 copy-start.31
  606.5 5.6 copy-start.37
  710.8 155.1 %copy-start.6 = (bf16[1,128,1024]{2,1,0:T(8,128)(2,1)S(1)}, bf16[1,128,1024]{2,1,0:T(8,128)(2,1)}, u32[]{:S(2)}) copy-start(bf16[1,128,1024]{2,1,0:T(8,128)(2,1)} %param.9) | copy-start | bytes 786436
  710.8 155.2 %copy-start.26 = (f32[4096]{0:T(1024)S(1)}, f32[4096]{0:T(1024)}, u32[]{:S(2)}) copy-start(f32[4096]{0:T(1024)} %get-tuple-element.114) | copy-start | bytes 49156
  710.8 155.4 %copy-start.23 = (f32[1024]{0:T(1024)S(1)}, f32[1024]{0:T(1024)}, u32[]{:S(2)}) copy-start(f32[1024]{0:T(1024)} %get-tuple-element.58) | copy-start | bytes 12292
  710.8 155.4 %copy-start.24 = (f32[1024]{0:T(1024)S(1)}, f32[1024]{0:T(1024)}, u32[]{:S(2)}) copy-start(f32[1024]{0:T(1024)} %get-tuple-element.77) | copy-start | bytes 12292
  710.8 155.4 %copy-start.32 = (f32[1024]{0:T(1024)S(1)}, f32[1024]{0:T(1024)}, u32[]{:S(2)}) copy-start(f32[1024]{0:T(1024)} %get-tuple-element.56) | copy-start | bytes 12292
  710.9 155.4 %copy-start.33 = (f32[1024]{0:T(1024)S(1)}, f32[1024]{0:T(1024)}, u32[]{:S(2)}) copy-start(f32[1024]{0:T(1024)} %get-tuple-element.61) | copy-start | bytes 12292
  710.9 199.1 %copy-start.19 = (f32[12,1024]{1,0:T(8,128)S(1)}, f32[12,1024]{1,0:T(8,128)}, u32[]{:S(2)}) copy-start(f32[12,1024]{1,0:T(8,128)} %param.14) | copy-start | bytes 147460
  710.9 199.1 %copy-start.20 = (f32[12,1024]{1,0:T(8,128)S(1)}, f32[12,1024]{1,0:T(8,128)}, u32[]{:S(2)}) copy-start(f32[12,1024]{1,0:T(8,128)} %param.15) | copy-start | bytes 147460
  710.9 199.8 %copy-start.11 = (f32[128,1024]{1,0:T(8,128)S(1)}, f32[128,1024]{1,0:T(8,128)}, u32[]{:S(2)}) copy-start(f32[128,1024]{1,0:T(8,128)} %copy-done.10) | copy-start | bytes 1572868
  710.9 199.8 %copy-start.12 = (bf16[128,1024]{0,1:T(8,128)(2,1)S(1)}, bf16[128,1024]{0,1:T(8,128)(2,1)}, u32[]{:S(2)}) copy-start(bf16[128,1024]{0,1:T(8,128)(2,1)} %copy.21) | copy-start | bytes 786436
  710.9 199.8 %copy-start.13 = (bf16[128,16,64]{0,2,1:T(8,128)(2,1)S(1)}, bf16[128,16,64]{0,2,1:T(8,128)(2,1)}, u32[]{:S(2)}) copy-start(bf16[128,16,64]{0,2,1:T(8,128)(2,1)} %get-tuple-element.93) | copy-start | bytes 786436
  710.9 279.1 %all-reduce.2.cloned.1.call-start = ((), (), s32[]{:S(2)}) async-start(), calls=%async_computation.6 | async-start | bytes 6291456 | tf_op jit(solution)/shard_map/psum | solution.py:340
  910.0 5.3 copy-start.18
Sparse Core Ops, SparseCore 0:
  489.7 31.1 all-gather.2
  523.0 28.2 all-gather.4
  592.6 25.5 reduce-scatter.11
  621.0 25.7 reduce-scatter.9
  711.0 154.7 reduce-scatter.7
  868.1 121.9 all-reduce.1
